TPU v7x, 32 devices: a whole 2x2x4 slice. The times are simulated.
32 devices in a mesh: dom: 8 (over z, x), band: 4 (over y, core).
Axes of the slice: x: 2, y: 2, z: 4, core: 2. Of those that a mesh axis runs over, the one named last changes fastest.
Arguments:
- orbitals: float32 [32, 96, 64, 128], P('band', 'dom'), may hold values from -1400 to 1400
- potential: float32 [96, 64, 128], P('dom'), may hold values from 0.1 to 2
Outputs:
- ortho_orbitals: float32 [32, 96, 64, 128], P('band', 'dom')
All inputs are finite; a program needn't handle non-finite values.
Results may differ from a plain program's by a relative error of at most 0.0003.
Values sent between devices are 32-bit elements; how exact they have to be, the bound alone decides.
A program may use at most 64 MiB of HBM per device.

v0:
```python
import jax
import jax.numpy as jnp
from jax import lax
from jax.sharding import PartitionSpec as P

stencil_weights = [
    -5369.0 / 1800.0,
    12.0 / 7.0,
    -15.0 / 56.0,
    10.0 / 189.0,
    -1.0 / 112.0,
    2.0 / 1925.0,
    -1.0 / 16632.0,
]
center_shift = 9.5
half_width = 7.5


def padded_2(block, sides, width):
    for axis, dim in sides:
        count = lax.axis_size(axis)
        forward = [(i, i + 1) for i in range(count - 1)]
        backward = [(target, source) for source, target in forward]
        low = lax.ppermute(
            lax.slice_in_dim(block, block.shape[dim] - width, None, axis=dim), axis, forward
        )
        high = lax.ppermute(lax.slice_in_dim(block, 0, width, axis=dim), axis, backward)
        block = jnp.concatenate([low, block, high], axis=dim)
    return block


def apply_hamiltonian(padded, field_potential):
    length = field_potential.shape[0]
    inner = padded[:, 6 : 6 + length]
    rows_y = inner.shape[2]
    rows_z = inner.shape[3]
    spread = jnp.pad(inner, ((0, 0), (0, 0), (6, 6), (6, 6)))
    laplace = 3.0 * stencil_weights[0] * inner
    for offset in range(1, 7):
        near = (
            padded[:, 6 + offset : 6 + offset + length]
            + padded[:, 6 - offset : 6 - offset + length]
        )
        near = (
            near
            + spread[:, :, 6 + offset : 6 + offset + rows_y, 6 : 6 + rows_z]
            + spread[:, :, 6 - offset : 6 - offset + rows_y, 6 : 6 + rows_z]
        )
        near = (
            near
            + spread[:, :, 6 : 6 + rows_y, 6 + offset : 6 + offset + rows_z]
            + spread[:, :, 6 : 6 + rows_y, 6 - offset : 6 - offset + rows_z]
        )
        laplace = laplace + stencil_weights[offset] * near
    return -0.5 * laplace + field_potential * inner


def shards(orbitals, potential):
    own_rows = orbitals.shape[1]
    padded = padded_2(orbitals, (("dom", 1),), 6)
    first = (apply_hamiltonian(padded, potential) - center_shift * orbitals) / half_width
    padded_first = padded_2(first, (("dom", 1),), 6)
    filtered = (
        2.0 * (apply_hamiltonian(padded_first, potential) - center_shift * first) / half_width
        - orbitals
    )
    cells = lax.all_to_all(filtered, "band", split_axis=2, concat_axis=0, tiled=True)
    count = cells.shape[0]
    flat = cells.reshape(count, -1)
    partial_correlation = jnp.dot(
        flat, flat.T, precision=lax.Precision.HIGHEST, preferred_element_type=jnp.float32
    )
    all_cells = own_rows * lax.axis_size("dom") * orbitals.shape[2] * orbitals.shape[3]
    correlation = lax.psum(partial_correlation, ("dom", "band")) / jnp.float32(all_cells)
    lower = jnp.linalg.cholesky(correlation)
    inverse = lax.linalg.triangular_solve(
        lower, jnp.eye(count, dtype=correlation.dtype), left_side=True, lower=True
    )
    ortho = jnp.dot(
        inverse, flat, precision=lax.Precision.HIGHEST, preferred_element_type=jnp.float32
    ).reshape(cells.shape)
    return lax.all_to_all(ortho, "band", split_axis=0, concat_axis=2, tiled=True)


def solution(mesh):
    in_specs = (P("band", "dom", None, None), P("dom", None, None))
    out_specs = P("band", "dom", None, None)
    return jax.shard_map(shards, mesh=mesh, in_specs=in_specs, out_specs=out_specs, check_vma=False)
```

profile of v0, /device:TPU:0, one launch (start us, length us, event | category | flops | bytes accessed | tf_op | source)
XLA Modules:
  0.0 322.1 jit_solution(681666642300067285)
XLA Ops:
  0.0 2.2 fusion.103
  2.2 0.0 copy-start
  2.2 5.2 %collective-permute-start.1 = (f32[8,6,64,128]{3,2,1,0:T(8,128)S(1)}, f32[8,6,64,128]{3,2,1,0:T(8,128)S(1)}, u32[]{:S(2)}, u32[]{:S(2)}) collective-permute-start(f32[8,6,64,128]{3,2,1,0:T(8,128)S(1)} %get-tuple-element.10), channel_id=1, source_target_pairs={{0,4},{4,8},{8,12},{12,16},{16,20},{20,24},{24,28},{1,5},{5,9},{9,... | collective-permute-start | bytes 4718600 | tf_op jit(solution)/shard_map/ppermute | solution.py:24
  7.4 1.3 collective-permute-start
  8.7 65.9 %collective-permute-done.1 = f32[8,6,64,128]{3,2,1,0:T(8,128)S(1)} collective-permute-done((f32[8,6,64,128]{3,2,1,0:T(8,128)S(1)}, f32[8,6,64,128]{3,2,1,0:T(8,128)S(1)}, u32[]{:S(2)}, u32[]{:S(2)}) %collective-permute-start.1) | collective-permute-done | bytes 1572896 | tf_op jit(solution)/shard_map/ppermute | solution.py:24
  74.7 0.1 constant_dynamic-update-slice_fusion.3
  74.8 0.0 copy-done
  74.8 0.9 constant_dynamic-update-slice_fusion.1
  75.7 0.0 copy-start.3
  75.8 0.0 collective-permute-done
  75.8 0.2 constant_dynamic-update-slice_fusion
  75.9 0.8 copy-done.3
  76.7 11.5 %broadcast_multiply_fusion = (f32[8,12,64,128]{3,2,1,0:T(8,128)}, f32[8,12,64,128]{3,2,1,0:T(8,128)}) fusion(f32[8,12,64,128]{3,2,1,0:T(8,128)S(1)} %copy-done, f32[12,64,128]{2,1,0:T(8,128)S(1)} %copy-done.3, f32[8,18,64,128]{3,2,1,0:T(8,128)S(1)} %get-tuple-element.12, f32[8,18,64,128]{3,2,1,0:T(8,128)S(1)} %constant_dynamic-update-slice_fusion), kind=kLoop, calls=%fused_computation.175 | loop fusion | flops 38535168 | bytes 47579136 | tf_op jit(solution)/shard_map/div | solution.py:61
  88.2 0.0 copy-start.1
  88.2 0.0 copy-start.2
  88.2 2.3 fusion.102
  90.5 1.4 collective-permute-start.2
  91.9 5.1 %collective-permute-start.3 = (f32[8,6,64,128]{3,2,1,0:T(8,128)S(1)}, f32[8,6,64,128]{3,2,1,0:T(8,128)S(1)}, u32[]{:S(2)}, u32[]{:S(2)}) collective-permute-start(f32[8,6,64,128]{3,2,1,0:T(8,128)S(1)} %get-tuple-element.8), channel_id=1, source_target_pairs={{0,4},{4,8},{8,12},{12,16},{16,20},{20,24},{24,28},{1,5},{5,9},{9,... | collective-permute-start | bytes 4718600 | tf_op jit(solution)/shard_map/ppermute | solution.py:24
  97.1 31.5 %collective-permute-done.2 = f32[8,6,64,128]{3,2,1,0:T(8,128)S(1)} collective-permute-done((f32[8,6,64,128]{3,2,1,0:T(8,128)S(1)}, f32[8,6,64,128]{3,2,1,0:T(8,128)S(1)}, u32[]{:S(2)}, u32[]{:S(2)}) %collective-permute-start.2) | collective-permute-done | bytes 1572896 | tf_op jit(solution)/shard_map/ppermute | solution.py:27
  128.5 33.9 %collective-permute-done.3 = f32[8,6,64,128]{3,2,1,0:T(8,128)S(1)} collective-permute-done((f32[8,6,64,128]{3,2,1,0:T(8,128)S(1)}, f32[8,6,64,128]{3,2,1,0:T(8,128)S(1)}, u32[]{:S(2)}, u32[]{:S(2)}) %collective-permute-start.3) | collective-permute-done | bytes 1572896 | tf_op jit(solution)/shard_map/ppermute | solution.py:24
  162.4 0.0 copy-start.4
  162.4 1.1 copy-done.4
  163.5 0.0 copy-done.1
  163.5 0.0 copy-done.2
  163.5 11.9 %fusion.13 = f32[8,12,64,128]{3,2,1,0:T(8,128)S(1)} fusion(f32[8,12,64,128]{3,2,1,0:T(8,128)S(1)} %copy-done, f32[8,12,64,128]{3,2,1,0:T(8,128)S(1)} %copy-done.1, f32[8,6,64,128]{3,2,1,0:T(8,128)} %copy-done.4, f32[8,6,64,128]{3,2,1,0:T(8,128)S(1)} %collective-permute-done.2, f32[8,12,64,128]{3,2,1,0:T(8,128)S(1)} %copy-done.2, ...), kind=kLoop, calls=%fused_computation.81 | loop fusion | flops 48758784 | bytes 16121856 | tf_op jit(solution)/shard_map/sub | solution.py:64
  175.5 1.8 copy.28
  177.3 39.5 %all_to_all.33 = f32[8,12,64,128]{3,0,1,2:T(8,128)S(1)} all-to-all(f32[8,12,64,128]{3,0,1,2:T(8,128)S(1)} %copy.28), channel_id=1, replica_groups=mesh['dom'=8,'band'=4] {'band'}, dimensions={2} | all-to-all | bytes 6291456 | tf_op jit(solution)/shard_map/all_to_all | solution.py:67
  216.8 3.5 %copy.41 = f32[8,12,4,16,128]{4,3,1,0,2:T(8,128)} copy(f32[8,12,4,16,128]{4,0,1,3,2:T(8,128)S(1)} %bitcast.34) | data formatting | bytes 6291456 | tf_op jit(solution)/shard_map/all_to_all | solution.py:67
  220.3 2.2 reshape.16
  222.5 2.6 fusion.104
  225.1 40.6 %psum.7 = f32[32,32]{0,1:T(8,128)S(1)} all-reduce(f32[32,32]{0,1:T(8,128)S(1)} %fusion.104), channel_id=1, replica_groups=mesh['dom'=8,'band'=4] {'dom','band'}, use_global_device_ids=true, to_apply=%region_0.1 | all-reduce | flops 1024 | bytes 8192 | tf_op jit(solution)/shard_map/psum | solution.py:74
  265.7 0.1 copy.31
  265.8 2.9 cholesky.17
  268.7 0.6 compare_reduce_fusion
  269.4 0.7 fusion.98
  270.0 2.4 custom-call.6
  272.5 0.2 convolution_bitcast_fusion
  272.7 0.6 copy.37
  273.3 4.6 %fusion.96 = f32[32,12,16,128]{3,0,2,1:T(8,128)S(1)} fusion(f32[32,32,1,1]{1,0,3,2:T(8,128)S(1)} %convolution_bitcast_fusion, f32[12,16,128,32]{2,1,0,3:T(8,128)S(1)} %bitcast.33), kind=kOutput, calls=%fused_computation.172 | convolution fusion | flops 301989888 | bytes 6295552 | tf_op jit(solution)/shard_map/dot_general | solution.py:79
  277.9 1.8 copy.33
  279.7 40.3 %all_to_all.34 = f32[32,12,16,128]{3,2,1,0:T(8,128)S(1)} all-to-all(f32[32,12,16,128]{3,2,1,0:T(8,128)S(1)} %copy.33), channel_id=1, replica_groups=mesh['dom'=8,'band'=4] {'band'}, dimensions={0} | all-to-all | bytes 6291456 | tf_op jit(solution)/shard_map/all_to_all | solution.py:82
  320.0 2.1 copy.34
  (4 shorter events, 0.1 us)
Async XLA Ops:
  2.2 72.6 %copy-start = (f32[8,12,64,128]{3,2,1,0:T(8,128)S(1)}, f32[8,12,64,128]{3,2,1,0:T(8,128)}, u32[]{:S(2)}) copy-start(f32[8,12,64,128]{3,2,1,0:T(8,128)} %param.2) | copy-start | bytes 9437188
  2.2 72.5 %collective-permute-start.1 = (f32[8,6,64,128]{3,2,1,0:T(8,128)S(1)}, f32[8,6,64,128]{3,2,1,0:T(8,128)S(1)}, u32[]{:S(2)}, u32[]{:S(2)}) collective-permute-start(f32[8,6,64,128]{3,2,1,0:T(8,128)S(1)} %get-tuple-element.10), channel_id=1, source_target_pairs={{0,4},{4,8},{8,12},{12,16},{16,20},{20,24},{24,28},{1,5},{5,9},{9,... | collective-permute-start | bytes 4718600 | tf_op jit(solution)/shard_map/ppermute | solution.py:24
  7.4 68.3 %collective-permute-start = (f32[8,6,64,128]{3,2,1,0:T(8,128)S(1)}, f32[8,6,64,128]{3,2,1,0:T(8,128)S(1)}, u32[]{:S(2)}, u32[]{:S(2)}) collective-permute-start(f32[8,6,64,128]{3,2,1,0:T(8,128)S(1)} %get-tuple-element.9), channel_id=1, source_target_pairs={{4,0},{8,4},{12,8},{16,12},{20,16},{24,20},{28,24},{5,1},{9,5},{13... | collective-permute-start | bytes 4718600 | tf_op jit(solution)/shard_map/ppermute | solution.py:27
  75.7 1.0 copy-start.3
  88.2 75.3 %copy-start.1 = (f32[8,12,64,128]{3,2,1,0:T(8,128)S(1)}, f32[8,12,64,128]{3,2,1,0:T(8,128)}, u32[]{:S(2)}) copy-start(f32[8,12,64,128]{3,2,1,0:T(8,128)} %get-tuple-element.5) | copy-start | bytes 9437188
  88.2 75.3 %copy-start.2 = (f32[8,12,64,128]{3,2,1,0:T(8,128)S(1)}, f32[8,12,64,128]{3,2,1,0:T(8,128)}, u32[]{:S(2)}) copy-start(f32[8,12,64,128]{3,2,1,0:T(8,128)} %get-tuple-element.6) | copy-start | bytes 9437188
  90.5 38.1 %collective-permute-start.2 = (f32[8,6,64,128]{3,2,1,0:T(8,128)S(1)}, f32[8,6,64,128]{3,2,1,0:T(8,128)S(1)}, u32[]{:S(2)}, u32[]{:S(2)}) collective-permute-start(f32[8,6,64,128]{3,2,1,0:T(8,128)S(1)} %get-tuple-element.7), channel_id=1, source_target_pairs={{4,0},{8,4},{12,8},{16,12},{20,16},{24,20},{28,24},{5,1},{9,5},{13... | collective-permute-start | bytes 4718600 | tf_op jit(solution)/shard_map/ppermute | solution.py:27
  91.9 70.5 %collective-permute-start.3 = (f32[8,6,64,128]{3,2,1,0:T(8,128)S(1)}, f32[8,6,64,128]{3,2,1,0:T(8,128)S(1)}, u32[]{:S(2)}, u32[]{:S(2)}) collective-permute-start(f32[8,6,64,128]{3,2,1,0:T(8,128)S(1)} %get-tuple-element.8), channel_id=1, source_target_pairs={{0,4},{4,8},{8,12},{12,16},{16,20},{20,24},{24,28},{1,5},{5,9},{9,... | collective-permute-start | bytes 4718600 | tf_op jit(solution)/shard_map/ppermute | solution.py:24
  162.4 1.1 copy-start.4
where the time goes:
time: 323 us; the launch traced here: 322 us
  waiting for transfers between devices  131 us (41%)
  blocking collectives  120 us (37%)
  other arithmetic  30.1 us (9%)
  local copies, waits for them, and re-layouts  19.7 us (6%)
  starting transfers between devices  13.1 us (4%)
  matrix products  7.36 us (2%)
    ppermute x2, waiting for transfers between devices, padded_2(): lax.ppermute(lax.slice_in_dim(block, block.shape[dim] - width, None, axis...  99.8 us
    psum x1, blocking collectives, shards(): lax.psum(partial_correlation, ('dom', 'band')) / jnp.float32(all_cells)  40.6 us
    all_to_all x1, blocking collectives, shards(): lax.all_to_all(ortho, 'band', split_axis=0, concat_axis=2, tiled=True)  40.3 us
    all_to_all x1, blocking collectives, shards(): lax.all_to_all(filtered, 'band', split_axis=2, concat_axis=0, tiled=True)  39.5 us
    ppermute x2, waiting for transfers between devices, padded_2(): lax.ppermute(lax.slice_in_dim(block, 0, width, axis=dim), axis, backward)  31.5 us
    sub x1, other arithmetic, shards(): 2.0 * (apply_hamiltonian(padded_first, potential) - center_shift * first)  11.9 us
    div x1, other arithmetic, shards(): (apply_hamiltonian(padded, potential) - center_shift * orbitals) / half_w...  11.5 us
    ppermute x2, starting transfers between devices, padded_2(): lax.ppermute(lax.slice_in_dim(block, block.shape[dim] - width, None, axis...  10.3 us
  transfers between devices with their start and end apart: 4, of which 3 were waited for; matrix products, arithmetic and copies ran while one was open for 0% of the time, Pallas kernels for 0%

commit v1 on v0

--- a/solution.py
+++ b/solution.py
@@ -71,7 +71,9 @@
         flat, flat.T, precision=lax.Precision.HIGHEST, preferred_element_type=jnp.float32
     )
     all_cells = own_rows * lax.axis_size("dom") * orbitals.shape[2] * orbitals.shape[3]
-    correlation = lax.psum(partial_correlation, ("dom", "band")) / jnp.float32(all_cells)
+    correlation = jnp.sum(
+        lax.all_gather(partial_correlation, ("dom", "band")), axis=0
+    ) / jnp.float32(all_cells)
     lower = jnp.linalg.cholesky(correlation)
     inverse = lax.linalg.triangular_solve(
         lower, jnp.eye(count, dtype=correlation.dtype), left_side=True, lower=True

time: 323 us -> 325 us (level)
    all_gather x0 -> x1, blocking collectives: none -> 43.2 us  [shards(): lax.all_gather(partial_correlation, ('dom', 'band'))]
    psum x1 -> x0, blocking collectives: 40.6 us -> none  [shards(): lax.psum(partial_correlation, ('dom', 'band')) / jnp.float32(all_cells)]
where the time goes in v1:
time: 325 us
  waiting for transfers between devices  131 us (40%)
  blocking collectives  122 us (38%)
  other arithmetic  31.2 us (10%)
  local copies, waits for them, and re-layouts  19.8 us (6%)
  starting transfers between devices  13.1 us (4%)
  matrix products  7.36 us (2%)
    ppermute x2, waiting for transfers between devices, padded_2(): lax.ppermute(lax.slice_in_dim(block, block.shape[dim] - width, None, axis...  99.8 us
    all_gather x1, blocking collectives, shards(): lax.all_gather(partial_correlation, ('dom', 'band'))  43.2 us
    all_to_all x1, blocking collectives, shards(): lax.all_to_all(filtered, 'band', split_axis=2, concat_axis=0, tiled=True)  39.5 us
    all_to_all x1, blocking collectives, shards(): lax.all_to_all(ortho, 'band', split_axis=0, concat_axis=2, tiled=True)  39.4 us
    ppermute x2, waiting for transfers between devices, padded_2(): lax.ppermute(lax.slice_in_dim(block, 0, width, axis=dim), axis, backward)  31.5 us
    sub x1, other arithmetic, shards(): 2.0 * (apply_hamiltonian(padded_first, potential) - center_shift * first)  11.9 us
    div x1, other arithmetic, shards(): (apply_hamiltonian(padded, potential) - center_shift * orbitals) / half_w...  11.5 us
    ppermute x2, starting transfers between devices, padded_2(): lax.ppermute(lax.slice_in_dim(block, block.shape[dim] - width, None, axis...  10.3 us
  transfers between devices with their start and end apart: 4, of which 3 were waited for; matrix products, arithmetic and copies ran while one was open for 0% of the time, Pallas kernels for 0%

profile of v1, /device:TPU:0, one launch (start us, length us, event | category | flops | bytes accessed | tf_op | source)
XLA Modules:
  0.0 325.0 jit_solution(18360705173210993309)
XLA Ops:
  0.0 2.2 fusion.103
  2.2 0.0 copy-start
  2.2 5.2 %collective-permute-start.1 = (f32[8,6,64,128]{3,2,1,0:T(8,128)S(1)}, f32[8,6,64,128]{3,2,1,0:T(8,128)S(1)}, u32[]{:S(2)}, u32[]{:S(2)}) collective-permute-start(f32[8,6,64,128]{3,2,1,0:T(8,128)S(1)} %get-tuple-element.10), channel_id=1, source_target_pairs={{0,4},{4,8},{8,12},{12,16},{16,20},{20,24},{24,28},{1,5},{5,9},{9,... | collective-permute-start | bytes 4718600 | tf_op jit(solution)/shard_map/ppermute | solution.py:24
  7.4 1.3 collective-permute-start
  8.7 65.9 %collective-permute-done.1 = f32[8,6,64,128]{3,2,1,0:T(8,128)S(1)} collective-permute-done((f32[8,6,64,128]{3,2,1,0:T(8,128)S(1)}, f32[8,6,64,128]{3,2,1,0:T(8,128)S(1)}, u32[]{:S(2)}, u32[]{:S(2)}) %collective-permute-start.1) | collective-permute-done | bytes 1572896 | tf_op jit(solution)/shard_map/ppermute | solution.py:24
  74.7 0.1 constant_dynamic-update-slice_fusion.3
  74.8 0.0 copy-done
  74.8 0.9 constant_dynamic-update-slice_fusion.1
  75.7 0.0 copy-start.3
  75.8 0.0 collective-permute-done
  75.8 0.2 constant_dynamic-update-slice_fusion
  75.9 0.8 copy-done.3
  76.7 11.5 %broadcast_multiply_fusion = (f32[8,12,64,128]{3,2,1,0:T(8,128)}, f32[8,12,64,128]{3,2,1,0:T(8,128)}) fusion(f32[8,12,64,128]{3,2,1,0:T(8,128)S(1)} %copy-done, f32[12,64,128]{2,1,0:T(8,128)S(1)} %copy-done.3, f32[8,18,64,128]{3,2,1,0:T(8,128)S(1)} %get-tuple-element.12, f32[8,18,64,128]{3,2,1,0:T(8,128)S(1)} %constant_dynamic-update-slice_fusion), kind=kLoop, calls=%fused_computation.175 | loop fusion | flops 38535168 | bytes 47579136 | tf_op jit(solution)/shard_map/div | solution.py:61
  88.2 0.0 copy-start.1
  88.2 0.0 copy-start.2
  88.2 2.3 fusion.102
  90.5 1.4 collective-permute-start.2
  91.9 5.1 %collective-permute-start.3 = (f32[8,6,64,128]{3,2,1,0:T(8,128)S(1)}, f32[8,6,64,128]{3,2,1,0:T(8,128)S(1)}, u32[]{:S(2)}, u32[]{:S(2)}) collective-permute-start(f32[8,6,64,128]{3,2,1,0:T(8,128)S(1)} %get-tuple-element.8), channel_id=1, source_target_pairs={{0,4},{4,8},{8,12},{12,16},{16,20},{20,24},{24,28},{1,5},{5,9},{9,... | collective-permute-start | bytes 4718600 | tf_op jit(solution)/shard_map/ppermute | solution.py:24
  97.1 31.5 %collective-permute-done.2 = f32[8,6,64,128]{3,2,1,0:T(8,128)S(1)} collective-permute-done((f32[8,6,64,128]{3,2,1,0:T(8,128)S(1)}, f32[8,6,64,128]{3,2,1,0:T(8,128)S(1)}, u32[]{:S(2)}, u32[]{:S(2)}) %collective-permute-start.2) | collective-permute-done | bytes 1572896 | tf_op jit(solution)/shard_map/ppermute | solution.py:27
  128.5 33.9 %collective-permute-done.3 = f32[8,6,64,128]{3,2,1,0:T(8,128)S(1)} collective-permute-done((f32[8,6,64,128]{3,2,1,0:T(8,128)S(1)}, f32[8,6,64,128]{3,2,1,0:T(8,128)S(1)}, u32[]{:S(2)}, u32[]{:S(2)}) %collective-permute-start.3) | collective-permute-done | bytes 1572896 | tf_op jit(solution)/shard_map/ppermute | solution.py:24
  162.4 0.0 copy-start.4
  162.4 1.1 copy-done.4
  163.5 0.0 copy-done.1
  163.5 0.0 copy-done.2
  163.5 11.9 %fusion.13 = f32[8,12,64,128]{3,2,1,0:T(8,128)S(1)} fusion(f32[8,12,64,128]{3,2,1,0:T(8,128)S(1)} %copy-done, f32[8,12,64,128]{3,2,1,0:T(8,128)S(1)} %copy-done.1, f32[8,6,64,128]{3,2,1,0:T(8,128)} %copy-done.4, f32[8,6,64,128]{3,2,1,0:T(8,128)S(1)} %collective-permute-done.2, f32[8,12,64,128]{3,2,1,0:T(8,128)S(1)} %copy-done.2, ...), kind=kLoop, calls=%fused_computation.81 | loop fusion | flops 48758784 | bytes 16121856 | tf_op jit(solution)/shard_map/sub | solution.py:64
  175.5 1.8 copy.26
  177.3 39.5 %all_to_all.33 = f32[8,12,64,128]{3,0,1,2:T(8,128)S(1)} all-to-all(f32[8,12,64,128]{3,0,1,2:T(8,128)S(1)} %copy.26), channel_id=1, replica_groups=mesh['dom'=8,'band'=4] {'band'}, dimensions={2} | all-to-all | bytes 6291456 | tf_op jit(solution)/shard_map/all_to_all | solution.py:67
  216.8 3.5 %copy.38 = f32[8,12,4,16,128]{4,3,1,0,2:T(8,128)} copy(f32[8,12,4,16,128]{4,0,1,3,2:T(8,128)S(1)} %bitcast.35) | data formatting | bytes 6291456 | tf_op jit(solution)/shard_map/all_to_all | solution.py:67
  220.3 2.2 reshape.16
  222.5 2.6 fusion.104
  225.1 43.2 %all-gather = f32[1024,32]{1,0:T(8,128)} all-gather(f32[32,32]{1,0:T(8,128)S(1)} %fusion.104), channel_id=2, replica_groups=mesh['dom'=8,'band'=4] {'dom','band'}, dimensions={0}, use_global_device_ids=true | all-gather | bytes 135168 | tf_op jit(solution)/shard_map/all_gather | solution.py:75
  268.3 1.1 reduce_sum.9
  269.4 0.1 copy.28
  269.5 0.1 copy.29
  269.5 2.9 cholesky.17
  272.5 0.6 compare_reduce_fusion
  273.1 0.7 fusion.98
  273.8 2.4 custom-call.6
  276.2 0.2 convolution_bitcast_fusion
  276.5 0.6 copy.34
  277.0 4.6 %fusion.96 = f32[32,12,16,128]{3,0,2,1:T(8,128)S(1)} fusion(f32[32,32,1,1]{1,0,3,2:T(8,128)S(1)} %convolution_bitcast_fusion, f32[12,16,128,32]{2,1,0,3:T(8,128)S(1)} %bitcast.34), kind=kOutput, calls=%fused_computation.172 | convolution fusion | flops 301989888 | bytes 6295552 | tf_op jit(solution)/shard_map/dot_general | solution.py:81
  281.6 1.8 copy.31
  283.4 39.4 %all_to_all.34 = f32[32,12,16,128]{3,2,1,0:T(8,128)S(1)} all-to-all(f32[32,12,16,128]{3,2,1,0:T(8,128)S(1)} %copy.31), channel_id=1, replica_groups=mesh['dom'=8,'band'=4] {'band'}, dimensions={0} | all-to-all | bytes 6291456 | tf_op jit(solution)/shard_map/all_to_all | solution.py:84
  322.9 2.1 copy.32
  (4 shorter events, 0.1 us)
Async XLA Ops:
  2.2 72.6 %copy-start = (f32[8,12,64,128]{3,2,1,0:T(8,128)S(1)}, f32[8,12,64,128]{3,2,1,0:T(8,128)}, u32[]{:S(2)}) copy-start(f32[8,12,64,128]{3,2,1,0:T(8,128)} %param.2) | copy-start | bytes 9437188
  2.2 72.5 %collective-permute-start.1 = (f32[8,6,64,128]{3,2,1,0:T(8,128)S(1)}, f32[8,6,64,128]{3,2,1,0:T(8,128)S(1)}, u32[]{:S(2)}, u32[]{:S(2)}) collective-permute-start(f32[8,6,64,128]{3,2,1,0:T(8,128)S(1)} %get-tuple-element.10), channel_id=1, source_target_pairs={{0,4},{4,8},{8,12},{12,16},{16,20},{20,24},{24,28},{1,5},{5,9},{9,... | collective-permute-start | bytes 4718600 | tf_op jit(solution)/shard_map/ppermute | solution.py:24
  7.4 68.3 %collective-permute-start = (f32[8,6,64,128]{3,2,1,0:T(8,128)S(1)}, f32[8,6,64,128]{3,2,1,0:T(8,128)S(1)}, u32[]{:S(2)}, u32[]{:S(2)}) collective-permute-start(f32[8,6,64,128]{3,2,1,0:T(8,128)S(1)} %get-tuple-element.9), channel_id=1, source_target_pairs={{4,0},{8,4},{12,8},{16,12},{20,16},{24,20},{28,24},{5,1},{9,5},{13... | collective-permute-start | bytes 4718600 | tf_op jit(solution)/shard_map/ppermute | solution.py:27
  75.7 1.0 copy-start.3
  88.2 75.3 %copy-start.1 = (f32[8,12,64,128]{3,2,1,0:T(8,128)S(1)}, f32[8,12,64,128]{3,2,1,0:T(8,128)}, u32[]{:S(2)}) copy-start(f32[8,12,64,128]{3,2,1,0:T(8,128)} %get-tuple-element.5) | copy-start | bytes 9437188
  88.2 75.3 %copy-start.2 = (f32[8,12,64,128]{3,2,1,0:T(8,128)S(1)}, f32[8,12,64,128]{3,2,1,0:T(8,128)}, u32[]{:S(2)}) copy-start(f32[8,12,64,128]{3,2,1,0:T(8,128)} %get-tuple-element.6) | copy-start | bytes 9437188
  90.5 38.1 %collective-permute-start.2 = (f32[8,6,64,128]{3,2,1,0:T(8,128)S(1)}, f32[8,6,64,128]{3,2,1,0:T(8,128)S(1)}, u32[]{:S(2)}, u32[]{:S(2)}) collective-permute-start(f32[8,6,64,128]{3,2,1,0:T(8,128)S(1)} %get-tuple-element.7), channel_id=1, source_target_pairs={{4,0},{8,4},{12,8},{16,12},{20,16},{24,20},{28,24},{5,1},{9,5},{13... | collective-permute-start | bytes 4718600 | tf_op jit(solution)/shard_map/ppermute | solution.py:27
  91.9 70.5 %collective-permute-start.3 = (f32[8,6,64,128]{3,2,1,0:T(8,128)S(1)}, f32[8,6,64,128]{3,2,1,0:T(8,128)S(1)}, u32[]{:S(2)}, u32[]{:S(2)}) collective-permute-start(f32[8,6,64,128]{3,2,1,0:T(8,128)S(1)} %get-tuple-element.8), channel_id=1, source_target_pairs={{0,4},{4,8},{8,12},{12,16},{16,20},{20,24},{24,28},{1,5},{5,9},{9,... | collective-permute-start | bytes 4718600 | tf_op jit(solution)/shard_map/ppermute | solution.py:24
  162.4 1.1 copy-start.4
